TPU v7x, 32 devices: a whole 2x2x4 slice. The times are simulated.
32 devices in a mesh: gx: 16 (over z, x, core), gy: 2 (over y).
Axes of the slice: x: 2, y: 2, z: 4, core: 2. Of those that a mesh axis runs over, the one named last changes fastest.
Arguments:
- particles: float32 [64, 2, 64, 1024], P(None, None, 'gx', 'gy'), may hold values from -32 to 32, as said below
- background: float32 [2, 64, 1024], P(None, 'gx', 'gy'), may hold values from -6 to 6
- obs_tile: int32 [16, 256], P('gx', 'gy'), may hold values from 0 to 127
- obs_mask: int32 [16, 16, 256], P(None, 'gx', 'gy'), may hold values 0 or 1
- obs_value: float32 [16, 256], P('gx', 'gy'), may hold values from -6 to 6
- obs_var: float32 [16, 256], P('gx', 'gy'), may hold values from 0.1 to 1
Outputs:
- analysis: float32 [64, 2, 64, 1024], P(None, None, 'gx', 'gy')
Inputs may be any that keep to these rules, and one draw needn't show every extreme that they name: `particles`: each particle is a field of order one to a few. `obs_tile`: an observation's value names tile row t // 128 and tile column t % (128) of its slab.
All inputs are finite; a program needn't handle non-finite values. No bound on the sum of `obs_mask` on one device may be relied on, other than what follows from the above.
Results may differ from a plain program's by a relative error of at most 0.0001.
Values sent between devices are 32-bit elements; how exact they have to be, the bound alone decides.
A program may use at most 64 MiB of HBM per device.

v0:
```python
import jax
import jax.numpy as jnp
from jax import lax
from jax.sharding import PartitionSpec as P

STEPS = 2
TILE = 4
lap_weight = 0.25
prior_weight = 0.05
couple_weight = 0.5
step_length = 1.0
epsilon = 1e-06
highest = lax.Precision.HIGHEST


def with_halo(block, sides, width):
    for axis, dim in sides:
        count = lax.axis_size(axis)
        forward = [(i, i + 1) for i in range(count - 1)]
        forward.append((count - 1, 0))
        backward = [(target, source) for source, target in forward]
        low = lax.ppermute(
            lax.slice_in_dim(block, block.shape[dim] - width, None, axis=dim), axis, forward
        )
        high = lax.ppermute(lax.slice_in_dim(block, 0, width, axis=dim), axis, backward)
        block = jnp.concatenate([low, block, high], axis=dim)
    return block


def laplace_inner(field):
    total = field[..., 1:-1, 2:] + field[..., 1:-1, :-2]
    total = total + field[..., 2:, 1:-1] + field[..., :-2, 1:-1]
    return total - 4.0 * field[..., 1:-1, 1:-1]


def prior_term(deviation):
    padded = with_halo(deviation, (("gx", 2), ("gy", 3)), 2)
    smooth = padded[..., 1:-1, 1:-1] - lap_weight * laplace_inner(padded)
    curved = smooth[..., 1:-1, 1:-1] - lap_weight * laplace_inner(smooth)
    return -prior_weight * (curved + couple_weight * (deviation - deviation[:, ::-1]))


def observe_term(state, table, weights, values, variance):
    count, rows, cols = (state.shape[0], state.shape[2], state.shape[3])
    tile_rows, tile_cols = (rows // TILE, cols // TILE)
    upper = state[:, 0].reshape(count, tile_rows, TILE, tile_cols, TILE)
    cells = upper.transpose(2, 4, 0, 1, 3).reshape(TILE * TILE, count, tile_rows * tile_cols)
    picked = jnp.einsum("cpt,ot->cpo", cells, table, precision=highest)
    mapped = 0.25 * jnp.sum(weights[:, None, :] * picked, axis=0)
    innovation = (values[None, :] - mapped) / variance[None, :]
    contrib = (0.25 * weights)[:, None, :] * innovation[None]
    spread = jnp.einsum("cpo,ot->cpt", contrib, table, precision=highest)
    back = spread.reshape(TILE, TILE, count, tile_rows, tile_cols).transpose(2, 3, 0, 4, 1)
    back = back.reshape(count, rows, cols)
    return jnp.stack([back, jnp.zeros_like(back)], axis=1)


def norm_scale(drift, denominator):
    total = lax.psum(jnp.sum(drift * drift), ("gx", "gy"))
    return step_length / jnp.sqrt(total / denominator + epsilon)


def per_device(particles, background, obs_tile, obs_mask, obs_value, obs_var):
    count = particles.shape[0]
    tiles = particles.shape[2] // TILE * (particles.shape[3] // TILE)
    table = (obs_tile[0][:, None] == jnp.arange(tiles, dtype=jnp.int32)[None, :]).astype(
        jnp.float32
    )
    weights = obs_mask[:, 0, :].astype(jnp.float32)
    values = obs_value[0]
    variance = obs_var[0]
    local_size = particles[0].size
    total_size = float(local_size * lax.axis_size("gx") * lax.axis_size("gy"))
    pair_count = float(count * (count - 1))
    off_diag = 1.0 - jnp.eye(count, dtype=jnp.float32)
    state = particles
    gram = None
    for step in range(STEPS):
        deviation = state - background[None]
        flat_dev = deviation.reshape(count, -1)
        if gram is None:
            gram = lax.psum(jnp.dot(flat_dev, flat_dev.T, precision=highest), ("gx", "gy"))
        gradient = prior_term(deviation) + observe_term(state, table, weights, values, variance)
        flat_grad = gradient.reshape(count, -1)
        diagonal = jnp.diagonal(gram)
        distance = diagonal[:, None] + diagonal[None, :] - 2.0 * gram
        width = jnp.sum(distance * off_diag) / (pair_count * total_size) + epsilon
        kernel = jnp.exp(-distance / (2.0 * width * total_size))
        attract = jnp.dot(kernel, flat_grad, precision=highest)
        pulled = jnp.dot(kernel, flat_dev, precision=highest)
        drift = (attract + (jnp.sum(kernel, axis=1)[:, None] * flat_dev - pulled) / width) / count
        if step + 1 < STEPS:
            cross, square = lax.psum(
                (
                    jnp.dot(flat_dev, drift.T, precision=highest),
                    jnp.dot(drift, drift.T, precision=highest),
                ),
                ("gx", "gy"),
            )
            scale = step_length / jnp.sqrt(jnp.trace(square) / (count * total_size) + epsilon)
            gram = gram + scale * (cross + cross.T) + scale * scale * square
        else:
            scale = norm_scale(drift, count * total_size)
        state = state + scale * drift.reshape(state.shape)
    return state


def solution(mesh):
    return jax.shard_map(
        per_device,
        mesh=mesh,
        in_specs=(
            P(None, None, "gx", "gy"),
            P(None, "gx", "gy"),
            P("gx", "gy"),
            P(None, "gx", "gy"),
            P("gx", "gy"),
            P("gx", "gy"),
        ),
        out_specs=P(None, None, "gx", "gy"),
        check_vma=False,
    )
```

profile of v0, /device:TPU:14, one launch (start us, length us, event | category | flops | bytes accessed | tf_op | source)
XLA Modules:
  0.0 223.9 jit_solution(16743643375088304163)
XLA Ops:
  0.0 2.8 %copy.40 = f32[64,2,4,512]{0,3,2,1:T(8,128)} copy(f32[64,2,4,512]{3,2,1,0:T(4,128)} %param.6) | data formatting | bytes 2097152 | tf_op args[0]
  2.8 2.2 broadcast_subtract_fusion.1
  6.1 2.4 %copy.32 = f32[64,2,2,512]{3,0,2,1:T(8,128)} copy(f32[64,2,2,512]{0,3,2,1:T(8,128)} %get-tuple-element.15) | data formatting | bytes 1048576 | tf_op jit(solution)/shard_map/slice | solution.py:23
  9.6 1.7 collective-permute-start.1
  11.3 1.9 slice.112
  13.2 3.6 %convolution_bitcast_fusion.1 = f32[64,64]{1,0:T(8,128)S(1)} fusion(f32[64,2,4,512]{0,3,2,1:T(8,128)S(1)} %broadcast_subtract_fusion.1), kind=kOutput, calls=%fused_computation.61 | convolution fusion | flops 201326592 | bytes 1064960 | tf_op jit(solution)/shard_map/dot_general | solution.py:82
  19.3 41.9 %psum.28 = f32[64,64]{1,0:T(8,128)S(1)} all-reduce(f32[64,64]{1,0:T(8,128)S(1)} %convolution_bitcast_fusion.1), channel_id=1, replica_groups=mesh['gx'=16,'gy'=2] {'gx','gy'}, use_global_device_ids=true, to_apply=%region_0.0 | all-reduce | flops 4096 | bytes 32768 | tf_op jit(solution)/shard_map/psum | solution.py:82
  64.2 1.5 fusion.26
  65.7 3.4 %fusion.1 = f32[64,4096]{1,0:T(8,128)} fusion(f32[64,4096]{0,1:T(8,128)S(1)} %bitcast.63, f32[64,4096]{1,0:T(8,128)S(1)} %copy.57, f32[]{:T(128)S(6)} %add.128, f32[64]{0:T(128)S(1)} %fusion.55, f32[64,64]{1,0:T(8,128)S(1)} %psum.28, f32[]{:T(128)S(6)} %mul.175, f32[64]{0:T(128)S(1)} %gather_fusion), kind=kOutput, calls=%fused_computation.6 | convolution fusion | flops 202133504 | bytes 3162632 | tf_op jit(solution)/shard_map/dot_general | solution.py:90
  70.5 2.4 %copy.35 = f32[64,2,2,512]{0,3,2,1:T(8,128)} copy(f32[64,2,2,512]{3,0,2,1:T(8,128)} %collective-permute-done.1) | data formatting | bytes 1048576 | tf_op jit(solution)/shard_map/ppermute | solution.py:25
  73.8 1.9 collective-permute-start.3
  77.0 2.4 %copy.38 = f32[4,4,64,1,128]{2,1,4,0,3:T(4,128)} copy(f32[4,4,64,1,128]{4,2,1,0,3:T(8,128)} %bitcast.78) | data formatting | bytes 1048576 | tf_op jit(solution)/shard_map/reshape | solution.py:53
  79.4 1.8 pad_maximum_fusion
  81.1 2.2 %fusion.8 = f32[64,2,6,514]{0,3,2,1:T(8,128)S(1)} fusion(f32[64,2,8,516]{0,3,2,1:T(8,128)S(1)} %pad_maximum_fusion, f32[64,2,8,2]{0,3,2,1:T(2,128)S(1)} %collective-permute-done.2, f32[64,2,2,512]{0,3,2,1:T(8,128)S(1)} %copy-done.1, f32[64,2,4,512]{0,3,2,1:T(8,128)S(1)} %broadcast_subtract_fusion.1, f32[64,2,2,512]{0,3,2,1:T(8,128)S(1)} %copy.34, ...), kind=kLoop, calls=%fused_computation.25 | loop fusion | flops 5131776 | bytes 8429568 | tf_op jit(solution)/shard_map/sub | solution.py:38
  84.6 2.4 %convolution_add_fusion.1 = f32[64,4096]{1,0:T(8,128)S(1)} fusion(f32[64,4096]{1,0:T(8,128)S(1)} %copy-done.3, f32[64,4096]{0,1:T(8,128)S(1)} %bitcast.67, f32[64,64]{1,0:T(8,128)S(1)} %psum.28, f32[]{:T(128)S(6)} %mul.175, f32[64]{0:T(128)S(1)} %gather_fusion), kind=kOutput, calls=%fused_computation.7 | convolution fusion | flops 201609216 | bytes 3162372 | tf_op jit(solution)/shard_map/dot_general | solution.py:89
  87.1 1.5 fusion.27
  89.6 39.4 %all-reduce.2 = (f32[64,64]{1,0:T(8,128)S(1)}, f32[64,64]{0,1:T(8,128)S(1)}) all-reduce(f32[64,64]{1,0:T(8,128)S(1)} %fusion.29, f32[64,64]{0,1:T(8,128)S(1)} %fusion.27), channel_id=1, replica_groups=mesh['gx'=16,'gy'=2] {'gx','gy'}, use_global_device_ids=true, to_apply=%region_4.5 | all-reduce | flops 8192 | bytes 65536 | tf_op jit(solution)/shard_map/psum | solution.py:93
  130.4 1.9 copy.58
  132.3 3.5 %broadcast_subtract_fusion = (f32[64,2,4,512]{0,3,2,1:T(8,128)S(1)}, f32[64,2,4,512]{0,3,2,1:T(8,128)}) fusion(f32[2,4,512]{2,1,0:T(4,128)S(1)} %copy-done.7, f32[64,2,4,512]{0,3,2,1:T(8,128)} %copy.40, f32[64,2,4,512]{0,3,2,1:T(8,128)} %bitcast.70), kind=kLoop, calls=%fused_computation.63 | loop fusion | flops 524288 | bytes 4210688 | tf_op jit(solution)/shard_map/sub | solution.py:79
  136.9 2.4 %copy.44 = f32[64,2,2,512]{3,0,2,1:T(8,128)} copy(f32[64,2,2,512]{0,3,2,1:T(8,128)} %get-tuple-element.13) | data formatting | bytes 1048576 | tf_op jit(solution)/shard_map/slice | solution.py:23
  140.4 1.7 collective-permute-start.5
  144.5 1.5 fusion.25
  149.1 3.4 %fusion = f32[64,4096]{1,0:T(8,128)} fusion(f32[64,4096]{0,1:T(8,128)S(1)} %bitcast.66, f32[64,4096]{1,0:T(8,128)S(1)} %copy.59, f32[]{:T(128)S(6)} %add.146, f32[64]{0:T(128)S(1)} %fusion.56, f32[64,64]{1,0:T(8,128)S(1)} %fusion.48, f32[]{:T(128)S(6)} %mul.204, f32[64]{0:T(128)S(1)} %gather_fusion.1), kind=kOutput, calls=%fused_computation.3 | convolution fusion | flops 202133504 | bytes 3162632 | tf_op jit(solution)/shard_map/dot_general | solution.py:90
  155.2 2.4 %copy.47 = f32[64,2,2,512]{0,3,2,1:T(8,128)} copy(f32[64,2,2,512]{3,0,2,1:T(8,128)} %collective-permute-done.5) | data formatting | bytes 1048576 | tf_op jit(solution)/shard_map/ppermute | solution.py:25
  161.6 2.4 %copy.49 = f32[4,4,64,1,128]{2,1,4,0,3:T(4,128)} copy(f32[4,4,64,1,128]{4,2,1,0,3:T(8,128)} %bitcast.77) | data formatting | bytes 1048576 | tf_op jit(solution)/shard_map/reshape | solution.py:53
  164.0 1.7 pad_maximum_fusion.1
  165.8 2.2 %fusion.4 = f32[64,2,6,514]{0,3,2,1:T(8,128)S(1)} fusion(f32[64,2,8,516]{0,3,2,1:T(8,128)S(1)} %pad_maximum_fusion.1, f32[64,2,8,2]{0,3,2,1:T(2,128)S(1)} %collective-permute-done.6, f32[64,2,2,512]{0,3,2,1:T(8,128)S(1)} %copy-done, f32[64,2,4,512]{0,3,2,1:T(8,128)S(1)} %get-tuple-element.7, f32[64,2,2,512]{0,3,2,1:T(8,128)S(1)} %copy.46, ...), kind=kLoop, calls=%fused_computation.13 | loop fusion | flops 5131776 | bytes 8429568 | tf_op jit(solution)/shard_map/sub | solution.py:38
  169.3 3.1 %multiply_reduce_fusion = (f32[]{:T(128)}, f32[64,4096]{1,0:T(8,128)S(1)}) fusion(f32[64,4096]{1,0:T(8,128)S(1)} %copy-done.4, f32[64,4096]{0,1:T(8,128)S(1)} %bitcast.69, f32[64,64]{1,0:T(8,128)S(1)} %fusion.48, f32[]{:T(128)S(6)} %mul.204, f32[64]{0:T(128)S(1)} %gather_fusion.1), kind=kOutput, calls=%fused_computation.62 | convolution fusion | flops 202395648 | bytes 3162376 | tf_op jit(solution)/shard_map/dot_general | solution.py:89
  172.3 43.0 %psum.31 = f32[]{:T(128)} all-reduce(f32[]{:T(128)} %get-tuple-element.17), channel_id=1, replica_groups=mesh['gx'=16,'gy'=2] {'gx','gy'}, use_global_device_ids=true, to_apply=%region_11.12 | all-reduce | flops 1 | bytes 8 | tf_op jit(solution)/shard_map/psum | solution.py:59
  216.2 1.9 copy.60
  218.1 3.2 %add.157 = f32[64,2,4,512]{0,3,2,1:T(8,128)} add(f32[64,2,4,512]{0,3,2,1:T(8,128)S(1)} %copy-done.2, f32[64,2,4,512]{0,3,2,1:T(8,128)} %bitcast.68) | non-fusion elementwise | flops 262144 | bytes 3145728 | tf_op jit(solution)/shard_map/add | solution.py:104
  221.2 2.7 %copy.52 = f32[64,2,4,512]{3,2,1,0:T(4,128)} copy(f32[64,2,4,512]{0,3,2,1:T(8,128)} %add.157) | data formatting | bytes 2097152 | tf_op jit(solution)/shard_map/add | solution.py:104
  (72 shorter events, 28.5 us)
Async XLA Ops:
  0.0 2.8 %copy-start.7 = (f32[2,4,512]{2,1,0:T(4,128)S(1)}, f32[2,4,512]{2,1,0:T(4,128)}, u32[]{:S(2)}) copy-start(f32[2,4,512]{2,1,0:T(4,128)} %param.7) | copy-start | bytes 49156
  8.5 60.7 %collective-permute-start = (f32[64,2,2,512]{3,0,2,1:T(8,128)}, f32[64,2,2,512]{3,0,2,1:T(8,128)}, u32[]{:S(2)}, u32[]{:S(2)}) collective-permute-start(f32[64,2,2,512]{3,0,2,1:T(8,128)} %copy.32), channel_id=1, source_target_pairs={{0,2},{2,4},{4,6},{6,8},{8,10},{10,12},{12,14},{14,16},{16,18},{18... | collective-permute-start | bytes 1572872 | tf_op jit(solution)/shard_map/ppermute | solution.py:22
  9.6 60.9 %collective-permute-start.1 = (f32[64,2,2,512]{3,0,2,1:T(8,128)}, f32[64,2,2,512]{3,0,2,1:T(8,128)}, u32[]{:S(2)}, u32[]{:S(2)}) collective-permute-start(f32[64,2,2,512]{3,0,2,1:T(8,128)} %copy.33), channel_id=1, source_target_pairs={{2,0},{4,2},{6,4},{8,6},{10,8},{12,10},{14,12},{16,14},{18,16},{20... | collective-permute-start | bytes 1572872 | tf_op jit(solution)/shard_map/ppermute | solution.py:25
  13.2 3.6 %copy-start.8 = (s32[16,1,128]{2,1,0:T(1,128)S(1)}, s32[16,1,128]{2,1,0:T(1,128)}, u32[]{:S(2)}) copy-start(s32[16,1,128]{2,1,0:T(1,128)} %param.9) | copy-start | bytes 24580
  19.3 44.8 %copy-start.9 = (s32[1,128]{1,0:T(1,128)S(1)}, s32[1,128]{1,0:T(1,128)}, u32[]{:S(2)}) copy-start(s32[1,128]{1,0:T(1,128)} %param.8) | copy-start | bytes 1540
  61.2 4.5 %copy-start.10 = (f32[1,128]{1,0:T(1,128)S(1)}, f32[1,128]{1,0:T(1,128)}, u32[]{:S(2)}) copy-start(f32[1,128]{1,0:T(1,128)} %param.11) | copy-start | bytes 1540
  61.2 4.4 %copy-start.11 = (f32[1,128]{1,0:T(1,128)S(1)}, f32[1,128]{1,0:T(1,128)}, u32[]{:S(2)}) copy-start(f32[1,128]{1,0:T(1,128)} %param.10) | copy-start | bytes 1540
  73.7 5.7 %collective-permute-start.2 = (f32[64,2,8,2]{0,3,2,1:T(2,128)S(1)}, f32[64,2,8,2]{0,3,2,1:T(2,128)S(1)}, u32[]{:S(2)}, u32[]{:S(2)}) collective-permute-start(f32[64,2,8,2]{0,3,2,1:T(2,128)S(1)} %get-tuple-element.11), channel_id=1, source_target_pairs={{0,1},{1,0},{2,3},{3,2},{4,5},{5,4},{6,7},{7,6},{8,9},{9,8},{10,11... | collective-permute-start | bytes 24584 | tf_op jit(solution)/shard_map/ppermute | solution.py:22
  73.8 5.5 %collective-permute-start.3 = (f32[64,2,8,2]{0,3,2,1:T(2,128)S(1)}, f32[64,2,8,2]{0,3,2,1:T(2,128)S(1)}, u32[]{:S(2)}, u32[]{:S(2)}) collective-permute-start(f32[64,2,8,2]{0,3,2,1:T(2,128)S(1)} %get-tuple-element.12), channel_id=1, source_target_pairs={{1,0},{0,1},{3,2},{2,3},{5,4},{4,5},{7,6},{6,7},{9,8},{8,9},{11,10... | collective-permute-start | bytes 24584 | tf_op jit(solution)/shard_map/ppermute | solution.py:25
  79.3 1.8 copy-start.1
  81.1 2.3 %copy-start.6 = (f32[4,4,64,1,128]{2,1,4,0,3:T(4,128)S(1)}, f32[4,4,64,1,128]{2,1,4,0,3:T(4,128)}, u32[]{:S(2)}) copy-start(f32[4,4,64,1,128]{2,1,4,0,3:T(4,128)} %copy.38) | copy-start | bytes 1572868
  83.4 1.2 copy-start.3
  139.3 14.5 %collective-permute-start.4 = (f32[64,2,2,512]{3,0,2,1:T(8,128)}, f32[64,2,2,512]{3,0,2,1:T(8,128)}, u32[]{:S(2)}, u32[]{:S(2)}) collective-permute-start(f32[64,2,2,512]{3,0,2,1:T(8,128)} %copy.44), channel_id=1, source_target_pairs={{0,2},{2,4},{4,6},{6,8},{8,10},{10,12},{12,14},{14,16},{16,18},{18... | collective-permute-start | bytes 1572872 | tf_op jit(solution)/shard_map/ppermute | solution.py:22
  140.4 14.8 %collective-permute-start.5 = (f32[64,2,2,512]{3,0,2,1:T(8,128)}, f32[64,2,2,512]{3,0,2,1:T(8,128)}, u32[]{:S(2)}, u32[]{:S(2)}) collective-permute-start(f32[64,2,2,512]{3,0,2,1:T(8,128)} %copy.45), channel_id=1, source_target_pairs={{2,0},{4,2},{6,4},{8,6},{10,8},{12,10},{14,12},{16,14},{18,16},{20... | collective-permute-start | bytes 1572872 | tf_op jit(solution)/shard_map/ppermute | solution.py:25
  158.3 5.7 %collective-permute-start.6 = (f32[64,2,8,2]{0,3,2,1:T(2,128)S(1)}, f32[64,2,8,2]{0,3,2,1:T(2,128)S(1)}, u32[]{:S(2)}, u32[]{:S(2)}) collective-permute-start(f32[64,2,8,2]{0,3,2,1:T(2,128)S(1)} %get-tuple-element.9), channel_id=1, source_target_pairs={{0,1},{1,0},{2,3},{3,2},{4,5},{5,4},{6,7},{7,6},{8,9},{9,8},{10,11... | collective-permute-start | bytes 24584 | tf_op jit(solution)/shard_map/ppermute | solution.py:22
  159.6 4.4 %collective-permute-start.7 = (f32[64,2,8,2]{0,3,2,1:T(2,128)S(1)}, f32[64,2,8,2]{0,3,2,1:T(2,128)S(1)}, u32[]{:S(2)}, u32[]{:S(2)}) collective-permute-start(f32[64,2,8,2]{0,3,2,1:T(2,128)S(1)} %get-tuple-element.10), channel_id=1, source_target_pairs={{1,0},{0,1},{3,2},{2,3},{5,4},{4,5},{7,6},{6,7},{9,8},{8,9},{11,10... | collective-permute-start | bytes 24584 | tf_op jit(solution)/shard_map/ppermute | solution.py:25
  164.0 1.8 copy-start
  165.8 2.3 %copy-start.5 = (f32[4,4,64,1,128]{2,1,4,0,3:T(4,128)S(1)}, f32[4,4,64,1,128]{2,1,4,0,3:T(4,128)}, u32[]{:S(2)}) copy-start(f32[4,4,64,1,128]{2,1,4,0,3:T(4,128)} %copy.49) | copy-start | bytes 1572868
  168.0 1.2 copy-start.4
  216.1 1.9 copy-start.2
where the time goes:
time: 225 us; the launch traced here: 224 us
  blocking collectives  124 us (55%)
  local copies, waits for them, and re-layouts  40.5 us (18%)
  matrix products  23.9 us (11%)
  other arithmetic  23.2 us (10%)
  starting transfers between devices  7.67 us (3%)
  between operations  3.05 us (1%)
    psum x1, blocking collectives, norm_scale(): total = lax.psum(jnp.sum(drift * drift), ('gx', 'gy'))  43 us
    psum x1, blocking collectives, per_device(): lax.psum(jnp.dot(flat_dev, flat_dev.T, precision=highest), ('gx', 'gy'))  41.9 us
    psum x1, blocking collectives, per_device(): lax.psum((jnp.dot(flat_dev, drift.T, precision=highest), jnp.dot(drift, d...  39.4 us
    slice x4, local copies, waits for them, and re-layouts, with_halo(): lax.slice_in_dim(block, block.shape[dim] - width, None, axis=dim)  6.94 us
    dot_general x2, matrix products, per_device(): pulled = jnp.dot(kernel, flat_dev, precision=highest)  6.85 us
    ppermute x4, starting transfers between devices, with_halo(): lax.ppermute(lax.slice_in_dim(block, 0, width, axis=dim), axis, backward)  6.21 us
    sub x2, other arithmetic, per_device(): deviation = state - background[None]  5.68 us
    dot_general x2, matrix products, per_device(): attract = jnp.dot(kernel, flat_grad, precision=highest)  5.5 us
  transfers between devices with their start and end apart: 8, of which 1 were waited for; matrix products, arithmetic and copies ran while one was open for 17% of the time, Pallas kernels for 0%

commit v1 on v0

--- a/solution.py
+++ b/solution.py
@@ -90,12 +90,18 @@
         pulled = jnp.dot(kernel, flat_dev, precision=highest)
         drift = (attract + (jnp.sum(kernel, axis=1)[:, None] * flat_dev - pulled) / width) / count
         if step + 1 < STEPS:
-            cross, square = lax.psum(
+
+            def recast_the_waves(vals, group_axis, mesh_name):
+                z1 = lax.psum(vals, axis_name=group_axis)
+                return lax.psum(z1, axis_name=mesh_name)
+
+            cross, square = recast_the_waves(
                 (
                     jnp.dot(flat_dev, drift.T, precision=highest),
                     jnp.dot(drift, drift.T, precision=highest),
                 ),
-                ("gx", "gy"),
+                "gy",
+                "gx",
             )
             scale = step_length / jnp.sqrt(jnp.trace(square) / (count * total_size) + epsilon)
             gram = gram + scale * (cross + cross.T) + scale * scale * square

time: 225 us -> 250 us (1.11)
  blocking collectives: 124 us -> 148 us
    psum x1 -> x2, blocking collectives: 39.4 us -> 52.6 us  [the longest x1 45 us: recast_the_waves(): return lax.psum(z1, axis_name=mesh_name)]
    psum x1, blocking collectives: 43 us -> 53.2 us  [norm_scale(): total = lax.psum(jnp.sum(drift * drift), ('gx', 'gy'))]
  transfers between devices with their start and end apart: 8 -> 8, of which waited for: 1 -> 1; matrix products, arithmetic and copies ran while one was open for 17% -> 15% of each run, Pallas kernels for 0% -> 0%
where the time goes in v1:
time: 250 us; the launch traced here: 247 us
  blocking collectives  148 us (59%)
  local copies, waits for them, and re-layouts  40.5 us (16%)
  matrix products  23.9 us (10%)
  other arithmetic  23.2 us (9%)
  starting transfers between devices  7.67 us (3%)
  between operations  3.05 us (1%)
    psum x1, blocking collectives, norm_scale(): total = lax.psum(jnp.sum(drift * drift), ('gx', 'gy'))  53.2 us
    psum x1, blocking collectives, recast_the_waves(): return lax.psum(z1, axis_name=mesh_name)  45 us
    psum x1, blocking collectives, per_device(): lax.psum(jnp.dot(flat_dev, flat_dev.T, precision=highest), ('gx', 'gy'))  41.9 us
    psum x1, blocking collectives, recast_the_waves(): z1 = lax.psum(vals, axis_name=group_axis)  7.58 us
    slice x4, local copies, waits for them, and re-layouts, with_halo(): lax.slice_in_dim(block, block.shape[dim] - width, None, axis=dim)  6.92 us
    dot_general x2, matrix products, per_device(): pulled = jnp.dot(kernel, flat_dev, precision=highest)  6.85 us
    ppermute x4, starting transfers between devices, with_halo(): lax.ppermute(lax.slice_in_dim(block, 0, width, axis=dim), axis, backward)  5.78 us
    sub x2, other arithmetic, per_device(): deviation = state - background[None]  5.68 us
  transfers between devices with their start and end apart: 8, of which 1 were waited for; matrix products, arithmetic and copies ran while one was open for 15% of the time, Pallas kernels for 0%

profile of v1, /device:TPU:14, one launch (start us, length us, event | category | flops | bytes accessed | tf_op | source)
XLA Modules:
  0.0 247.2 jit_solution(18200161593746304538)
XLA Ops:
  0.0 2.8 %copy.40 = f32[64,2,4,512]{0,3,2,1:T(8,128)} copy(f32[64,2,4,512]{3,2,1,0:T(4,128)} %param.6) | data formatting | bytes 2097152 | tf_op args[0]
  2.8 2.2 broadcast_subtract_fusion.1
  6.1 2.4 copy.32
  9.6 1.7 collective-permute-start.1
  11.3 1.9 slice.112
  13.2 3.6 %convolution_bitcast_fusion.1 = f32[64,64]{1,0:T(8,128)S(1)} fusion(f32[64,2,4,512]{0,3,2,1:T(8,128)S(1)} %broadcast_subtract_fusion.1), kind=kOutput, calls=%fused_computation.61 | convolution fusion | flops 201326592 | bytes 1064960 | tf_op jit(solution)/shard_map/dot_general | solution.py:82
  19.3 41.9 %psum.42 = f32[64,64]{1,0:T(8,128)S(1)} all-reduce(f32[64,64]{1,0:T(8,128)S(1)} %convolution_bitcast_fusion.1), channel_id=1, replica_groups=mesh['gx'=16,'gy'=2] {'gx','gy'}, use_global_device_ids=true, to_apply=%region_0.0 | all-reduce | flops 4096 | bytes 32768 | tf_op jit(solution)/shard_map/psum | solution.py:82
  65.7 3.4 %fusion.1 = f32[64,4096]{1,0:T(8,128)} fusion(f32[64,4096]{0,1:T(8,128)S(1)} %bitcast.63, f32[64,4096]{1,0:T(8,128)S(1)} %copy.57, f32[]{:T(128)S(6)} %add.132, f32[64]{0:T(128)S(1)} %fusion.55, f32[64,64]{1,0:T(8,128)S(1)} %psum.42, f32[]{:T(128)S(6)} %mul.175, f32[64]{0:T(128)S(1)} %gather_fusion), kind=kOutput, calls=%fused_computation.6 | convolution fusion | flops 202133504 | bytes 3162632 | tf_op jit(solution)/shard_map/dot_general | solution.py:90
  70.5 2.4 copy.35
  73.8 2.0 collective-permute-start.3
  77.0 2.4 copy.38
  79.3 1.8 pad_maximum_fusion
  81.1 2.2 fusion.8
  84.6 2.4 convolution_add_fusion.1
  87.1 1.5 fusion.27
  89.6 7.6 %all-reduce.3 = (f32[64,64]{1,0:T(8,128)S(1)}, f32[64,64]{0,1:T(8,128)S(1)}) all-reduce(f32[64,64]{1,0:T(8,128)S(1)} %fusion.29, f32[64,64]{0,1:T(8,128)S(1)} %fusion.27), channel_id=1, replica_groups=mesh['gx'=16,'gy'=2] {'gy'}, use_global_device_ids=true, to_apply=%region_4.5 | all-reduce | flops 8192 | bytes 65536 | tf_op jit(solution)/shard_map/psum | solution.py:95
  97.2 45.0 %all-reduce.2 = (f32[64,64]{1,0:T(8,128)S(1)}, f32[64,64]{0,1:T(8,128)S(1)}) all-reduce(f32[64,64]{1,0:T(8,128)S(1)} %get-tuple-element.7, f32[64,64]{0,1:T(8,128)S(1)} %get-tuple-element.8), channel_id=1, replica_groups=mesh['gx'=16,'gy'=2] {'gx'}, use_global_device_ids=true, to_apply=%region_5.6 | all-reduce | flops 8192 | bytes 65536 | tf_op jit(solution)/shard_map/psum | solution.py:96
  143.5 1.9 copy.58
  145.4 3.5 %broadcast_subtract_fusion = (f32[64,2,4,512]{0,3,2,1:T(8,128)S(1)}, f32[64,2,4,512]{0,3,2,1:T(8,128)}) fusion(f32[2,4,512]{2,1,0:T(4,128)S(1)} %copy-done.7, f32[64,2,4,512]{0,3,2,1:T(8,128)} %copy.40, f32[64,2,4,512]{0,3,2,1:T(8,128)} %bitcast.70), kind=kLoop, calls=%fused_computation.63 | loop fusion | flops 524288 | bytes 4210688 | tf_op jit(solution)/shard_map/sub | solution.py:79
  150.0 2.4 copy.44
  153.5 1.7 collective-permute-start.5
  162.2 3.4 %fusion = f32[64,4096]{1,0:T(8,128)} fusion(f32[64,4096]{0,1:T(8,128)S(1)} %bitcast.66, f32[64,4096]{1,0:T(8,128)S(1)} %copy.59, f32[]{:T(128)S(6)} %add.150, f32[64]{0:T(128)S(1)} %fusion.56, f32[64,64]{1,0:T(8,128)S(1)} %fusion.48, f32[]{:T(128)S(6)} %mul.204, f32[64]{0:T(128)S(1)} %gather_fusion.1), kind=kOutput, calls=%fused_computation.3 | convolution fusion | flops 202133504 | bytes 3162632 | tf_op jit(solution)/shard_map/dot_general | solution.py:90
  168.3 2.4 copy.47
  171.4 1.8 collective-permute-start.6
  174.8 2.4 copy.49
  177.1 1.7 pad_maximum_fusion.1
  178.9 2.2 fusion.4
  182.4 3.1 %multiply_reduce_fusion = (f32[]{:T(128)}, f32[64,4096]{1,0:T(8,128)S(1)}) fusion(f32[64,4096]{1,0:T(8,128)S(1)} %copy-done.4, f32[64,4096]{0,1:T(8,128)S(1)} %bitcast.69, f32[64,64]{1,0:T(8,128)S(1)} %fusion.48, f32[]{:T(128)S(6)} %mul.204, f32[64]{0:T(128)S(1)} %gather_fusion.1), kind=kOutput, calls=%fused_computation.62 | convolution fusion | flops 202395648 | bytes 3162376 | tf_op jit(solution)/shard_map/dot_general | solution.py:89
  185.5 53.2 %psum.47 = f32[]{:T(128)} all-reduce(f32[]{:T(128)} %get-tuple-element.19), channel_id=1, replica_groups=mesh['gx'=16,'gy'=2] {'gx','gy'}, use_global_device_ids=true, to_apply=%region_13.14 | all-reduce | flops 1 | bytes 8 | tf_op jit(solution)/shard_map/psum | solution.py:59
  239.4 1.9 copy.60
  241.3 3.2 %add.161 = f32[64,2,4,512]{0,3,2,1:T(8,128)} add(f32[64,2,4,512]{0,3,2,1:T(8,128)S(1)} %copy-done.2, f32[64,2,4,512]{0,3,2,1:T(8,128)} %bitcast.68) | non-fusion elementwise | flops 262144 | bytes 3145728 | tf_op jit(solution)/shard_map/add | solution.py:110
  244.5 2.7 %copy.52 = f32[64,2,4,512]{3,2,1,0:T(4,128)} copy(f32[64,2,4,512]{0,3,2,1:T(8,128)} %add.161) | data formatting | bytes 2097152 | tf_op jit(solution)/shard_map/add | solution.py:110
  (73 shorter events, 29.7 us)
Async XLA Ops:
  0.0 2.8 %copy-start.7 = (f32[2,4,512]{2,1,0:T(4,128)S(1)}, f32[2,4,512]{2,1,0:T(4,128)}, u32[]{:S(2)}) copy-start(f32[2,4,512]{2,1,0:T(4,128)} %param.7) | copy-start | bytes 49156
  8.5 60.7 %collective-permute-start = (f32[64,2,2,512]{3,0,2,1:T(8,128)}, f32[64,2,2,512]{3,0,2,1:T(8,128)}, u32[]{:S(2)}, u32[]{:S(2)}) collective-permute-start(f32[64,2,2,512]{3,0,2,1:T(8,128)} %copy.32), channel_id=1, source_target_pairs={{0,2},{2,4},{4,6},{6,8},{8,10},{10,12},{12,14},{14,16},{16,18},{18... | collective-permute-start | bytes 1572872 | tf_op jit(solution)/shard_map/ppermute | solution.py:22
  9.6 60.9 %collective-permute-start.1 = (f32[64,2,2,512]{3,0,2,1:T(8,128)}, f32[64,2,2,512]{3,0,2,1:T(8,128)}, u32[]{:S(2)}, u32[]{:S(2)}) collective-permute-start(f32[64,2,2,512]{3,0,2,1:T(8,128)} %copy.33), channel_id=1, source_target_pairs={{2,0},{4,2},{6,4},{8,6},{10,8},{12,10},{14,12},{16,14},{18,16},{20... | collective-permute-start | bytes 1572872 | tf_op jit(solution)/shard_map/ppermute | solution.py:25
  13.2 3.6 %copy-start.8 = (s32[16,1,128]{2,1,0:T(1,128)S(1)}, s32[16,1,128]{2,1,0:T(1,128)}, u32[]{:S(2)}) copy-start(s32[16,1,128]{2,1,0:T(1,128)} %param.9) | copy-start | bytes 24580
  19.3 44.8 %copy-start.9 = (s32[1,128]{1,0:T(1,128)S(1)}, s32[1,128]{1,0:T(1,128)}, u32[]{:S(2)}) copy-start(s32[1,128]{1,0:T(1,128)} %param.8) | copy-start | bytes 1540
  61.2 4.5 %copy-start.10 = (f32[1,128]{1,0:T(1,128)S(1)}, f32[1,128]{1,0:T(1,128)}, u32[]{:S(2)}) copy-start(f32[1,128]{1,0:T(1,128)} %param.11) | copy-start | bytes 1540
  61.2 4.5 %copy-start.11 = (f32[1,128]{1,0:T(1,128)S(1)}, f32[1,128]{1,0:T(1,128)}, u32[]{:S(2)}) copy-start(f32[1,128]{1,0:T(1,128)} %param.10) | copy-start | bytes 1540
  73.7 5.7 %collective-permute-start.2 = (f32[64,2,8,2]{0,3,2,1:T(2,128)S(1)}, f32[64,2,8,2]{0,3,2,1:T(2,128)S(1)}, u32[]{:S(2)}, u32[]{:S(2)}) collective-permute-start(f32[64,2,8,2]{0,3,2,1:T(2,128)S(1)} %get-tuple-element.13), channel_id=1, source_target_pairs={{0,1},{1,0},{2,3},{3,2},{4,5},{5,4},{6,7},{7,6},{8,9},{9,8},{10,11... | collective-permute-start | bytes 24584 | tf_op jit(solution)/shard_map/ppermute | solution.py:22
  73.8 5.6 %collective-permute-start.3 = (f32[64,2,8,2]{0,3,2,1:T(2,128)S(1)}, f32[64,2,8,2]{0,3,2,1:T(2,128)S(1)}, u32[]{:S(2)}, u32[]{:S(2)}) collective-permute-start(f32[64,2,8,2]{0,3,2,1:T(2,128)S(1)} %get-tuple-element.14), channel_id=1, source_target_pairs={{1,0},{0,1},{3,2},{2,3},{5,4},{4,5},{7,6},{6,7},{9,8},{8,9},{11,10... | collective-permute-start | bytes 24584 | tf_op jit(solution)/shard_map/ppermute | solution.py:25
  79.3 1.8 copy-start.1
  81.1 2.3 copy-start.6
  83.4 1.2 copy-start.3
  152.4 14.5 %collective-permute-start.4 = (f32[64,2,2,512]{3,0,2,1:T(8,128)}, f32[64,2,2,512]{3,0,2,1:T(8,128)}, u32[]{:S(2)}, u32[]{:S(2)}) collective-permute-start(f32[64,2,2,512]{3,0,2,1:T(8,128)} %copy.44), channel_id=1, source_target_pairs={{0,2},{2,4},{4,6},{6,8},{8,10},{10,12},{12,14},{14,16},{16,18},{18... | collective-permute-start | bytes 1572872 | tf_op jit(solution)/shard_map/ppermute | solution.py:22
  153.5 14.8 %collective-permute-start.5 = (f32[64,2,2,512]{3,0,2,1:T(8,128)}, f32[64,2,2,512]{3,0,2,1:T(8,128)}, u32[]{:S(2)}, u32[]{:S(2)}) collective-permute-start(f32[64,2,2,512]{3,0,2,1:T(8,128)} %copy.45), channel_id=1, source_target_pairs={{2,0},{4,2},{6,4},{8,6},{10,8},{12,10},{14,12},{16,14},{18,16},{20... | collective-permute-start | bytes 1572872 | tf_op jit(solution)/shard_map/ppermute | solution.py:25
  171.4 5.7 %collective-permute-start.6 = (f32[64,2,8,2]{0,3,2,1:T(2,128)S(1)}, f32[64,2,8,2]{0,3,2,1:T(2,128)S(1)}, u32[]{:S(2)}, u32[]{:S(2)}) collective-permute-start(f32[64,2,8,2]{0,3,2,1:T(2,128)S(1)} %get-tuple-element.11), channel_id=1, source_target_pairs={{0,1},{1,0},{2,3},{3,2},{4,5},{5,4},{6,7},{7,6},{8,9},{9,8},{10,11... | collective-permute-start | bytes 24584 | tf_op jit(solution)/shard_map/ppermute | solution.py:22
  173.2 3.9 %collective-permute-start.7 = (f32[64,2,8,2]{0,3,2,1:T(2,128)S(1)}, f32[64,2,8,2]{0,3,2,1:T(2,128)S(1)}, u32[]{:S(2)}, u32[]{:S(2)}) collective-permute-start(f32[64,2,8,2]{0,3,2,1:T(2,128)S(1)} %get-tuple-element.12), channel_id=1, source_target_pairs={{1,0},{0,1},{3,2},{2,3},{5,4},{4,5},{7,6},{6,7},{9,8},{8,9},{11,10... | collective-permute-start | bytes 24584 | tf_op jit(solution)/shard_map/ppermute | solution.py:25
  177.1 1.8 copy-start
  178.9 2.3 copy-start.5
  181.2 1.2 copy-start.4
  239.4 1.9 copy-start.2
